TPU v7x, 32 devices: a whole 2x2x4 slice. The times are simulated.
32 devices in a mesh: grp: 2 (over x), bits: 16 (over z, y, core).
Axes of the slice: x: 2, y: 2, z: 4, core: 2. Of those that a mesh axis runs over, the one named last changes fastest.
Arguments:
- prefix: bfloat16 [128, 16, 1024], P(('grp', 'bits')), parts along dimension 0, may hold values from -6 to 6
- first_suffix: bfloat16 [8, 2, 512, 512], P('grp', None, 'bits'), parts along dimension 0, may hold values from -0.109375 to 0.109375
- pair_prefix: int32 [256, 3], P(('grp', 'bits')), parts along dimension 0, may hold values from 0 to 3
- pair_suffix: int32 [256, 3], P(('grp', 'bits')), parts along dimension 0, may hold values from 0 to 3, all different within a row
- merge_count: int32 [256], P(('grp', 'bits')), parts along dimension 0, may hold values from 1 to 3, as said below
- suffix: bfloat16 [32, 2, 512, 512], P(('grp', 'bits')), parts along dimension 0, may hold values from -0.1875 to 0.1875
- routes: int32 [256, 12], P(('grp', 'bits')), parts along dimension 0, may hold values from 0 to 15, all different within a row; in each aligned block of 8 rows (0 to 7, 8 to 15, ...) at most 8 rows name the same one
- cap: bfloat16 [2, 512, 64], replicated, may hold values from -0.0546875 to 0.0546875
Outputs:
- capped: float32 [256, 16, 128], P(('grp', 'bits')), parts along dimension 0
There are 2 independent parts, one for each index of `grp`. A program takes and returns all parts, laid end to end along the dimension named above; an argument that names none is the same for every part. Nothing has to cross between parts.
Inputs may be any that keep to these rules, and one draw needn't show every extreme that they name: `pair_suffix`: each row names 3 different lifetime-one blocks. `merge_count`: some piece has exactly 3 merges and some exactly one. `routes`: each row names 12 different suffixes; in each aligned block of 8 rows no suffix is named by more than 8 rows, a bound that some block reaches.
All inputs are finite; a program needn't handle non-finite values.
Results may differ from a plain program's by a relative error of at most 0.005.
Values may be sent and summed in bfloat16 or wider, within the bound.
A program may use at most 64 MiB of HBM per device.

v0:
```python
import jax
import jax.numpy as jnp
from jax import lax
from jax.sharding import PartitionSpec as P

HIGHEST_PRECISION = lax.Precision.HIGHEST


def complex_form(blocks):
    real_part = blocks[..., 0, :, :]
    imag_part = blocks[..., 1, :, :]
    upper_half = jnp.concatenate([real_part, imag_part], axis=-1)
    lower_half = jnp.concatenate([-imag_part, real_part], axis=-1)
    return jnp.concatenate([upper_half, lower_half], axis=-2)


def on_device(prefix, first_suffix, pair_prefix, pair_suffix, merge_count, suffix, routes, cap):
    pieces = pair_prefix.shape[0]
    merges = pair_prefix.shape[1]
    held_blocks = prefix.shape[0]
    rows_piece = prefix.shape[1]
    twice_width = prefix.shape[2]
    half_width = twice_width // 2
    first_count = first_suffix.shape[0]
    listed = routes.shape[1]
    owners = lax.axis_size("bits")
    slot_count = min(pieces, max(2, (2 * pieces * listed + owners - 1) // owners))
    live_mask = lax.broadcasted_iota(jnp.int32, (pieces, merges), 1) < merge_count[:, None]
    matches = (
        pair_suffix[:, :, None] == lax.broadcasted_iota(jnp.int32, (pieces, merges, first_count), 2)
    ) & live_mask[:, :, None]
    which_block = pair_prefix[:, :, None] == lax.broadcasted_iota(
        jnp.int32, (pieces, merges, held_blocks), 2
    )
    prefix_picks = jnp.einsum(
        "ika,ikp->iap", matches.astype(jnp.float32), which_block.astype(jnp.float32)
    ).astype(jnp.bfloat16)
    selected = jnp.einsum(
        "iap,prc->airc", prefix_picks, prefix, preferred_element_type=jnp.float32
    ).astype(jnp.bfloat16)
    selected = selected.reshape(first_count, pieces * rows_piece, twice_width)
    portion = lax.all_gather(first_suffix, "bits", axis=2, tiled=True)
    count_rows = portion.shape[2]
    real_cols = lax.slice_in_dim(selected, 0, count_rows, axis=2)
    imag_cols = lax.dynamic_slice_in_dim(selected, half_width, count_rows, 2)
    left_side = jnp.concatenate([real_cols, imag_cols], axis=2)
    upper_half = jnp.concatenate([portion[:, 0], portion[:, 1]], axis=2)
    lower_half = jnp.concatenate([-portion[:, 1], portion[:, 0]], axis=2)
    right_side = jnp.concatenate([upper_half, lower_half], axis=1)
    state_rows = jnp.einsum(
        "arc,acw->rw", left_side, right_side, preferred_element_type=jnp.float32
    )
    state_rows = state_rows.astype(jnp.bfloat16).reshape(pieces, rows_piece, twice_width)
    named_by = jnp.sum(
        (routes[:, :, None] == lax.broadcasted_iota(jnp.int32, (pieces, listed, owners), 2)).astype(
            jnp.int32
        ),
        axis=1,
    )
    slot_rank = jnp.cumsum(named_by, axis=0) - named_by
    slot_hit = (
        slot_rank[:, :, None] == lax.broadcasted_iota(jnp.int32, (pieces, owners, slot_count), 2)
    ) & (named_by[:, :, None] > 0)
    dispatch = jnp.transpose(slot_hit, (1, 2, 0)).astype(jnp.bfloat16)
    outgoing = jnp.einsum(
        "dmi,irc->dmrc", dispatch, state_rows, preferred_element_type=jnp.float32
    ).astype(jnp.bfloat16)
    own_form = complex_form(suffix[0])
    cap_form = complex_form(cap)
    products = jnp.einsum(
        "smrc,cw->smrw",
        lax.all_to_all(outgoing, "bits", split_axis=0, concat_axis=0, tiled=True),
        own_form,
        preferred_element_type=jnp.float32,
    ).astype(jnp.bfloat16)
    capped_terms = jnp.einsum(
        "smrw,wv->smrv", products, cap_form, preferred_element_type=jnp.float32
    )
    returned = lax.all_to_all(
        capped_terms.astype(jnp.bfloat16), "bits", split_axis=0, concat_axis=0, tiled=True
    ).astype(capped_terms.dtype)
    return jnp.einsum(
        "dmi,dmrv->irv", dispatch.astype(jnp.float32), returned, precision=HIGHEST_PRECISION
    )


def solution(mesh):
    return jax.shard_map(
        on_device,
        mesh=mesh,
        in_specs=(
            P(("grp", "bits"), None, None),
            P("grp", None, "bits", None),
            P(("grp", "bits"), None),
            P(("grp", "bits"), None),
            P(("grp", "bits")),
            P(("grp", "bits"), None, None, None),
            P(("grp", "bits"), None),
            P(),
        ),
        out_specs=P(("grp", "bits"), None, None),
        check_vma=False,
    )
```

profile of v0, /device:TPU:0, one launch (start us, length us, event | category | flops | bytes accessed | tf_op | source)
XLA Modules:
  0.0 205.2 jit_solution(14975206516049845053)
XLA Ops:
  6.5 0.0 all-gather.2.cloned.1.call-start
  6.5 1.7 copy.52
  8.2 0.0 all-gather.2.cloned.1.call-update
  8.2 0.8 copy.47
  9.0 0.8 copy.48
  9.7 0.7 iota_compare_fusion.5
  10.5 0.2 fusion.32
  10.7 1.3 fusion.22
  12.0 0.6 copy.51
  12.6 0.8 copy.46
  13.3 0.1 convert_reduce_fusion
  13.5 49.2 %all-gather.2.cloned.1.call-done = bf16[4,2,512,512]{3,2,0,1:T(8,128)(2,1)} async-done(((bf16[4,2,32,512]{3,2,0,1:T(8,128)(2,1)}), bf16[4,2,512,512]{3,2,0,1:T(8,128)(2,1)}) %all-gather.2.cloned.1.call-update) | async-done | bytes 4194320 | tf_op jit(solution)/shard_map/all_gather | solution.py:42
  62.7 0.0 copy-start
  62.7 2.7 %slice_bitcast_fusion = (bf16[4,512,512]{2,1,0:T(8,128)(2,1)S(1)}, bf16[4,512,512]{2,1,0:T(8,128)(2,1)S(1)}) fusion(bf16[4,2,512,512]{3,2,0,1:T(8,128)(2,1)} %all-gather.2.cloned.1.call-done), kind=kLoop, calls=%fused_computation.11 | loop fusion | bytes 8388608 | tf_op jit(solution)/shard_map/squeeze | solution.py:47
  65.3 0.8 copy-done
  66.1 0.1 fusion.63
  66.3 1.3 fusion.29
  67.6 1.6 convolution_convert_fusion
  69.1 4.3 %copy.54 = bf16[16,8,16,1024]{3,2,1,0:T(8,128)(2,1)} copy(bf16[16,8,16,1024]{3,0,2,1:T(8,128)(2,1)S(1)} %convolution_convert_fusion) | data formatting | bytes 8388608 | tf_op jit(solution)/shard_map/convert_element_type | solution.py:67
  73.4 0.0 copy-start.2
  73.4 0.0 copy-start.1
  73.4 4.9 %all-to-all-start = ((bf16[16,8,16,1024]{3,2,1,0:T(8,128)(2,1)}), bf16[16,8,16,1024]{3,2,1,0:T(8,128)(2,1)}, u32[]{:S(2)}, u32[]{:S(2)}) async-start(bf16[16,8,16,1024]{3,2,1,0:T(8,128)(2,1)} %copy.54), calls=%async_computation | async-start | bytes 8388608 | tf_op jit(solution)/shard_map/all_to_all | solution.py:72
  78.3 0.0 copy-done.2
  78.3 0.1 copy.68
  78.5 0.1 copy.67
  78.6 0.0 copy-done.1
  78.7 0.1 slice_bitcast_fusion.2
  78.7 76.9 %all-to-all-done = bf16[16,8,16,1024]{3,2,1,0:T(8,128)(2,1)} async-done(((bf16[16,8,16,1024]{3,2,1,0:T(8,128)(2,1)}), bf16[16,8,16,1024]{3,2,1,0:T(8,128)(2,1)}, u32[]{:S(2)}, u32[]{:S(2)}) %all-to-all-start) | async-done | bytes 4194336 | tf_op jit(solution)/shard_map/all_to_all | solution.py:72
  155.6 7.9 %fusion.23 = bf16[16,8,16,128]{3,2,1,0:T(8,128)(2,1)S(1)} fusion(bf16[16,8,16,1024]{3,2,1,0:T(8,128)(2,1)} %all-to-all-done, bf16[512,512]{1,0:T(8,128)(2,1)S(1)} %get-tuple-element.8, bf16[512,512]{1,0:T(8,128)(2,1)S(1)} %fusion.62, bf16[512,512]{1,0:T(8,128)(2,1)S(1)} %get-tuple-element.7, bf16[512,64]{1,0:T(8,128)(2,1)S(1)} %bitcast.66, ...), kind=kOutput, calls=%fused_computation.23 | convolution fusion | flops 4843634688 | bytes 6488064 | tf_op jit(solution)/shard_map/smrw,wv->smrv/dot_general | solution.py:76
  163.5 0.1 copy.57
  163.7 33.7 %all_to_all.10 = bf16[16,8,16,128]{3,1,2,0:T(8,128)(2,1)S(1)} all-to-all(bf16[16,8,16,128]{3,1,2,0:T(8,128)(2,1)S(1)} %copy.57), channel_id=1, replica_groups=mesh['grp'=2,'bits'=16] {'bits'}, dimensions={0} | all-to-all | bytes 1048576 | tf_op jit(solution)/shard_map/all_to_all | solution.py:79
  197.4 0.4 convolution_bitcast_fusion
  197.8 0.6 copy.59
  (6 shorter events, 0.1 us)
Async XLA Ops:
  6.5 56.1 %all-gather.2.cloned.1.call-start = ((), (), s32[]{:S(2)}) async-start(), calls=%async_computation.2 | async-start | bytes 4456448 | tf_op jit(solution)/shard_map/all_gather | solution.py:42
  62.7 3.4 %copy-start = (bf16[4,2,512,512]{3,2,0,1:T(8,128)(2,1)S(1)}, bf16[4,2,512,512]{3,2,0,1:T(8,128)(2,1)}, u32[]{:S(2)}) copy-start(bf16[4,2,512,512]{3,2,0,1:T(8,128)(2,1)} %all-gather.2.cloned.1.call-done) | copy-start | bytes 12582916
  73.4 4.9 %copy-start.2 = (bf16[2,512,64]{1,2,0:T(8,128)(2,1)S(1)}, bf16[2,512,64]{1,2,0:T(8,128)(2,1)}, u32[]{:S(2)}) copy-start(bf16[2,512,64]{1,2,0:T(8,128)(2,1)} %param.15) | copy-start | bytes 393220
  73.4 5.2 %copy-start.1 = (bf16[1,2,512,512]{3,2,1,0:T(8,128)(2,1)S(1)}, bf16[1,2,512,512]{3,2,1,0:T(8,128)(2,1)}, u32[]{:S(2)}) copy-start(bf16[1,2,512,512]{3,2,1,0:T(8,128)(2,1)} %param.13) | copy-start | bytes 3145732
  73.4 82.2 %all-to-all-start = ((bf16[16,8,16,1024]{3,2,1,0:T(8,128)(2,1)}), bf16[16,8,16,1024]{3,2,1,0:T(8,128)(2,1)}, u32[]{:S(2)}, u32[]{:S(2)}) async-start(bf16[16,8,16,1024]{3,2,1,0:T(8,128)(2,1)} %copy.54), calls=%async_computation | async-start | bytes 8388608 | tf_op jit(solution)/shard_map/all_to_all | solution.py:72
Sparse Core Ops, SparseCore 0:
  9.5 53.1 all-gather.1
where the time goes:
time: 206 us; the launch traced here: 205 us
  waiting for transfers between devices  126 us (61%)
  blocking collectives  33.7 us (16%)
  between operations  13.5 us (7%)
  local copies, waits for them, and re-layouts  13.4 us (7%)
  matrix products  12.7 us (6%)
  starting transfers between devices  4.85 us (2%)
    all_to_all x1, waiting for transfers between devices, on_device(): lax.all_to_all(outgoing, 'bits', split_axis=0, concat_axis=0, tiled=True)  76.9 us
    all_gather x1, waiting for transfers between devices, on_device(): portion = lax.all_gather(first_suffix, 'bits', axis=2, tiled=True)  49.2 us
    all_to_all x1, blocking collectives, on_device(): lax.all_to_all(capped_terms.astype(jnp.bfloat16), 'bits', split_axis=0, c...  33.7 us
    dot_general x1, matrix products, on_device(): jnp.einsum('smrw,wv->smrv', products, cap_form, preferred_element_type=jn...  7.92 us
    unnamed x12, local copies, waits for them, and re-layouts  4.98 us
    all_to_all x1, starting transfers between devices, on_device(): lax.all_to_all(outgoing, 'bits', split_axis=0, concat_axis=0, tiled=True)  4.85 us
    convert_element_type x1, local copies, waits for them, and re-layouts, on_device(): outgoing = jnp.einsum('dmi,irc->dmrc', dispatch, state_rows, preferred_el...  4.3 us
  transfers between devices with their start and end apart: 2, of which 2 were waited for; matrix products, arithmetic and copies ran while one was open for 3% of the time, Pallas kernels for 0%

commit v1 on v0

--- a/solution.py
+++ b/solution.py
@@ -2,8 +2,37 @@
 import jax.numpy as jnp
 from jax import lax
 from jax.sharding import PartitionSpec as P
+from jax.lax import axis_index, axis_size, ppermute
 
 HIGHEST_PRECISION = lax.Precision.HIGHEST
+
+
+def _draft_panels(arr, dim_i):
+    answer = list(arr.shape[1:])
+    answer[dim_i] *= arr.shape[0]
+    h_now = jnp.moveaxis(arr, 0, dim_i).reshape(answer)
+    return h_now
+
+
+def map_shapes_up(xs, mesh_ax, dim_no):
+    n_chips = axis_size(mesh_ax)
+    buffer = [(b, (b + 1) % n_chips) for b in range(n_chips)]
+    nodes = [(j0, c) for c, j0 in buffer]
+    shaped, carry_in = ([], [])
+    for src_i in range(n_chips - 1):
+        if src_i % 2 == 0:
+            ready = ppermute(shaped[-1] if shaped else xs, mesh_ax, buffer)
+            shaped.append(ready)
+        else:
+            m_next = ppermute(carry_in[-1] if carry_in else xs, mesh_ax, nodes)
+            carry_in.append(m_next)
+    q_next = jnp.stack([*shaped[::-1], xs, *carry_in], 0)
+    r1 = axis_index(mesh_ax)
+    p_next = len(shaped)
+    even = r1 - p_next
+    q_next = q_next[(jnp.arange(n_chips) - even) % n_chips]
+    part_next = _draft_panels(q_next, dim_no)
+    return part_next
 
 
 def complex_form(blocks):
@@ -39,7 +68,7 @@
         "iap,prc->airc", prefix_picks, prefix, preferred_element_type=jnp.float32
     ).astype(jnp.bfloat16)
     selected = selected.reshape(first_count, pieces * rows_piece, twice_width)
-    portion = lax.all_gather(first_suffix, "bits", axis=2, tiled=True)
+    portion = map_shapes_up(first_suffix, "bits", 2)
     count_rows = portion.shape[2]
     real_cols = lax.slice_in_dim(selected, 0, count_rows, axis=2)
     imag_cols = lax.dynamic_slice_in_dim(selected, half_width, count_rows, 2)

time: 206 us -> 228 us (1.11)
  starting transfers between devices: 4.85 us -> 37.5 us
  local copies, waits for them, and re-layouts: 13.4 us -> 33.5 us
  waiting for transfers between devices: 126 us -> 109 us
  between operations: 13.5 us -> 0.19 us
    all_gather x1 -> x0, waiting for transfers between devices: 49.2 us -> none  [on_device(): portion = lax.all_gather(first_suffix, 'bits', axis=2, tiled=True)]
    ppermute x0 -> x15, starting transfers between devices: none -> 32.6 us  [the longest x7 32.1 us: map_shapes_up(): m_next = ppermute(carry_in[-1] if carry_in else xs, mesh_ax, nodes)]
    ppermute x0 -> x15, waiting for transfers between devices: none -> 32.1 us  [the longest x8 27.7 us: map_shapes_up(): ready = ppermute(shaped[-1] if shaped else xs, mesh_ax, buffer)]
    unnamed x12 -> x30, local copies, waits for them, and re-layouts: 4.98 us -> 19.1 us
    gather x0 -> x1, local copies, waits for them, and re-layouts: none -> 4.99 us  [map_shapes_up(): q_next = q_next[(jnp.arange(n_chips) - even) % n_chips]]
    transpose x0 -> x1, local copies, waits for them, and re-layouts: none -> 2.66 us  [_draft_panels(): h_now = jnp.moveaxis(arr, 0, dim_i).reshape(answer)]
    squeeze x1, local copies, waits for them, and re-layouts: 2.65 us -> 0.27 us  [on_device(): upper_half = jnp.concatenate([portion[:, 0], portion[:, 1]], axis=2)]
  transfers between devices with their start and end apart: 2 -> 16, of which waited for: 2 -> 13; matrix products, arithmetic and copies ran while one was open for 3% -> 10% of each run, Pallas kernels for 0% -> 0%
where the time goes in v1:
time: 228 us
  waiting for transfers between devices  109 us (48%)
  starting transfers between devices  37.5 us (16%)
  blocking collectives  33.7 us (15%)
  local copies, waits for them, and re-layouts  33.5 us (15%)
  matrix products  12.7 us (6%)
    all_to_all x1, waiting for transfers between devices, on_device(): lax.all_to_all(outgoing, 'bits', split_axis=0, concat_axis=0, tiled=True)  76.9 us
    all_to_all x1, blocking collectives, on_device(): lax.all_to_all(capped_terms.astype(jnp.bfloat16), 'bits', split_axis=0, c...  33.7 us
    ppermute x7, starting transfers between devices, map_shapes_up(): m_next = ppermute(carry_in[-1] if carry_in else xs, mesh_ax, nodes)  32.1 us
    ppermute x8, waiting for transfers between devices, map_shapes_up(): ready = ppermute(shaped[-1] if shaped else xs, mesh_ax, buffer)  27.7 us
    unnamed x30, local copies, waits for them, and re-layouts  19.1 us
    dot_general x1, matrix products, on_device(): jnp.einsum('smrw,wv->smrv', products, cap_form, preferred_element_type=jn...  7.92 us
    gather x1, local copies, waits for them, and re-layouts, map_shapes_up(): q_next = q_next[(jnp.arange(n_chips) - even) % n_chips]  4.99 us
    all_to_all x1, starting transfers between devices, on_device(): lax.all_to_all(outgoing, 'bits', split_axis=0, concat_axis=0, tiled=True)  4.84 us
  transfers between devices with their start and end apart: 16, of which 13 were waited for; matrix products, arithmetic and copies ran while one was open for 10% of the time, Pallas kernels for 0%

profile of v1, /device:TPU:0, one launch (start us, length us, event | category | flops | bytes accessed | tf_op | source)
XLA Modules:
  0.0 227.6 jit_solution(16726823598896323727)
XLA Ops:
  0.5 9.3 %collective-permute-done = bf16[4,2,32,512]{3,2,1,0:T(8,128)(2,1)S(1)} collective-permute-done((bf16[4,2,32,512]{3,2,1,0:T(8,128)(2,1)}, bf16[4,2,32,512]{3,2,1,0:T(8,128)(2,1)S(1)}, u32[]{:S(2)}, u32[]{:S(2)}) %collective-permute-start) | collective-permute-done | bytes 262176 | tf_op jit(solution)/shard_map/ppermute | solution.py:24
  9.8 4.4 %collective-permute-start.8 = (bf16[4,2,32,512]{3,2,1,0:T(8,128)(2,1)}, bf16[4,2,32,512]{3,2,1,0:T(8,128)(2,1)S(1)}, u32[]{:S(2)}, u32[]{:S(2)}) collective-permute-start(bf16[4,2,32,512]{3,2,1,0:T(8,128)(2,1)} %param.9), channel_id=1, source_target_pairs={{1,0},{2,1},{3,2},{4,3},{5,4},{6,5},{7,6},{8,7},{9,8},{10,9},{11,1... | collective-permute-start | bytes 786440 | tf_op jit(solution)/shard_map/ppermute | solution.py:27
  14.3 4.1 %collective-permute-done.1 = bf16[4,2,32,512]{3,2,1,0:T(8,128)(2,1)S(1)} collective-permute-done((bf16[4,2,32,512]{3,2,1,0:T(8,128)(2,1)S(1)}, bf16[4,2,32,512]{3,2,1,0:T(8,128)(2,1)S(1)}, u32[]{:S(2)}, u32[]{:S(2)}) %collective-permute-start.1) | collective-permute-done | bytes 262176 | tf_op jit(solution)/shard_map/ppermute | solution.py:24
  18.5 4.6 %collective-permute-start.9 = (bf16[4,2,32,512]{3,2,1,0:T(8,128)(2,1)S(1)}, bf16[4,2,32,512]{3,2,1,0:T(8,128)(2,1)S(1)}, u32[]{:S(2)}, u32[]{:S(2)}) collective-permute-start(bf16[4,2,32,512]{3,2,1,0:T(8,128)(2,1)S(1)} %collective-permute-done.8), channel_id=1, source_target_pairs={{1,0},{2,1},{3,2},{4,3},{5,4},{6,5},{7,6},{8,7},{9,8},{10,9},{11,1... | collective-permute-start | bytes 786440 | tf_op jit(solution)/shard_map/ppermute | solution.py:27
  23.1 3.8 %collective-permute-done.2 = bf16[4,2,32,512]{3,2,1,0:T(8,128)(2,1)S(1)} collective-permute-done((bf16[4,2,32,512]{3,2,1,0:T(8,128)(2,1)S(1)}, bf16[4,2,32,512]{3,2,1,0:T(8,128)(2,1)S(1)}, u32[]{:S(2)}, u32[]{:S(2)}) %collective-permute-start.2) | collective-permute-done | bytes 262176 | tf_op jit(solution)/shard_map/ppermute | solution.py:24
  26.9 0.8 copy.46
  27.7 4.4 %collective-permute-start.10 = (bf16[4,2,32,512]{3,2,1,0:T(8,128)(2,1)S(1)}, bf16[4,2,32,512]{3,2,1,0:T(8,128)(2,1)S(1)}, u32[]{:S(2)}, u32[]{:S(2)}) collective-permute-start(bf16[4,2,32,512]{3,2,1,0:T(8,128)(2,1)S(1)} %collective-permute-done.9), channel_id=1, source_target_pairs={{1,0},{2,1},{3,2},{4,3},{5,4},{6,5},{7,6},{8,7},{9,8},{10,9},{11,1... | collective-permute-start | bytes 786440 | tf_op jit(solution)/shard_map/ppermute | solution.py:27
  32.1 3.4 %collective-permute-done.3 = bf16[4,2,32,512]{3,2,1,0:T(8,128)(2,1)S(1)} collective-permute-done((bf16[4,2,32,512]{3,2,1,0:T(8,128)(2,1)S(1)}, bf16[4,2,32,512]{3,2,1,0:T(8,128)(2,1)S(1)}, u32[]{:S(2)}, u32[]{:S(2)}) %collective-permute-start.3) | collective-permute-done | bytes 262176 | tf_op jit(solution)/shard_map/ppermute | solution.py:24
  35.6 0.8 copy.47
  36.3 0.8 copy.48
  37.1 0.7 iota_compare_fusion.5
  37.8 4.4 %collective-permute-start.11 = (bf16[4,2,32,512]{3,2,1,0:T(8,128)(2,1)S(1)}, bf16[4,2,32,512]{3,2,1,0:T(8,128)(2,1)S(1)}, u32[]{:S(2)}, u32[]{:S(2)}) collective-permute-start(bf16[4,2,32,512]{3,2,1,0:T(8,128)(2,1)S(1)} %collective-permute-done.10), channel_id=1, source_target_pairs={{1,0},{2,1},{3,2},{4,3},{5,4},{6,5},{7,6},{8,7},{9,8},{10,9},{11,1... | collective-permute-start | bytes 786440 | tf_op jit(solution)/shard_map/ppermute | solution.py:27
  42.3 1.8 collective-permute-done.4
  44.3 1.9 collective-permute-done.11
  46.2 4.7 %collective-permute-start.12 = (bf16[4,2,32,512]{3,2,1,0:T(8,128)(2,1)S(1)}, bf16[4,2,32,512]{3,2,1,0:T(8,128)(2,1)}, u32[]{:S(2)}, u32[]{:S(2)}) collective-permute-start(bf16[4,2,32,512]{3,2,1,0:T(8,128)(2,1)S(1)} %collective-permute-done.11), channel_id=1, source_target_pairs={{1,0},{2,1},{3,2},{4,3},{5,4},{6,5},{7,6},{8,7},{9,8},{10,9},{11,1... | collective-permute-start | bytes 786440 | tf_op jit(solution)/shard_map/ppermute | solution.py:27
  50.9 1.8 collective-permute-done.5
  52.7 1.4 fusion.22
  54.8 4.8 %collective-permute-start.13 = (bf16[4,2,32,512]{3,2,1,0:T(8,128)(2,1)}, bf16[4,2,32,512]{3,2,1,0:T(8,128)(2,1)}, u32[]{:S(2)}, u32[]{:S(2)}) collective-permute-start(bf16[4,2,32,512]{3,2,1,0:T(8,128)(2,1)} %collective-permute-done.12), channel_id=1, source_target_pairs={{1,0},{2,1},{3,2},{4,3},{5,4},{6,5},{7,6},{8,7},{9,8},{10,9},{11,1... | collective-permute-start | bytes 786440 | tf_op jit(solution)/shard_map/ppermute | solution.py:27
  59.6 1.8 collective-permute-done.6
  62.0 1.7 collective-permute-done.13
  63.8 4.7 %collective-permute-start.14 = (bf16[4,2,32,512]{3,2,1,0:T(8,128)(2,1)}, bf16[4,2,32,512]{3,2,1,0:T(8,128)(2,1)S(1)}, u32[]{:S(2)}, u32[]{:S(2)}) collective-permute-start(bf16[4,2,32,512]{3,2,1,0:T(8,128)(2,1)} %collective-permute-done.13), channel_id=1, source_target_pairs={{1,0},{2,1},{3,2},{4,3},{5,4},{6,5},{7,6},{8,7},{9,8},{10,9},{11,1... | collective-permute-start | bytes 786440 | tf_op jit(solution)/shard_map/ppermute | solution.py:27
  68.5 1.7 collective-permute-done.7
  70.2 1.7 bitcast_dynamic-update-slice_fusion.15
  71.9 1.7 bitcast_dynamic-update-slice_fusion.14
  73.5 1.7 bitcast_dynamic-update-slice_fusion.13
  75.2 1.7 bitcast_dynamic-update-slice_fusion.12
  76.8 0.7 bitcast_dynamic-update-slice_fusion.11
  77.6 0.7 bitcast_dynamic-update-slice_fusion.10
  78.3 0.7 bitcast_dynamic-update-slice_fusion.9
  79.0 0.7 bitcast_dynamic-update-slice_fusion.8
  79.8 0.7 bitcast_dynamic-update-slice_fusion.7
  80.5 0.7 bitcast_dynamic-update-slice_fusion.6
  81.2 0.7 bitcast_dynamic-update-slice_fusion.5
  82.0 0.7 bitcast_dynamic-update-slice_fusion.4
  82.7 0.7 bitcast_dynamic-update-slice_fusion.3
  83.4 1.7 bitcast_dynamic-update-slice_fusion.2
  85.1 1.7 bitcast_dynamic-update-slice_fusion.1
  86.8 0.7 bitcast_dynamic-update-slice_fusion
  87.5 5.0 %gather_fusion = bf16[16,4,2,32,512]{4,3,2,1,0:T(8,128)(2,1)} fusion(bf16[16,4,2,32,512]{4,3,2,1,0:T(8,128)(2,1)} %bitcast_dynamic-update-slice_fusion, s32[1024]{0:T(1024)S(1)} %pad_clamp_fusion), kind=kCustom, calls=%fused_computation | custom fusion | bytes 8388672 | tf_op jit(solution)/shard_map/gather | solution.py:33
  92.5 2.7 %copy.52 = bf16[4,2,16,32,512]{4,3,2,0,1:T(8,128)(2,1)S(1)} copy(bf16[4,2,16,32,512]{4,3,1,0,2:T(8,128)(2,1)} %bitcast.101) | data formatting | bytes 8388608 | tf_op jit(solution)/shard_map/transpose | solution.py:13
  95.5 1.3 fusion.29
  96.8 1.6 convolution_convert_fusion
  98.4 4.3 %copy.54 = bf16[16,8,16,1024]{3,2,1,0:T(8,128)(2,1)} copy(bf16[16,8,16,1024]{3,0,2,1:T(8,128)(2,1)S(1)} %convolution_convert_fusion) | data formatting | bytes 8388608 | tf_op jit(solution)/shard_map/convert_element_type | solution.py:96
  102.7 4.8 %all-to-all-start = ((bf16[16,8,16,1024]{3,2,1,0:T(8,128)(2,1)}), bf16[16,8,16,1024]{3,2,1,0:T(8,128)(2,1)}, u32[]{:S(2)}, u32[]{:S(2)}) async-start(bf16[16,8,16,1024]{3,2,1,0:T(8,128)(2,1)} %copy.54), calls=%async_computation | async-start | bytes 8388608 | tf_op jit(solution)/shard_map/all_to_all | solution.py:101
  108.0 76.9 %all-to-all-done = bf16[16,8,16,1024]{3,2,1,0:T(8,128)(2,1)} async-done(((bf16[16,8,16,1024]{3,2,1,0:T(8,128)(2,1)}), bf16[16,8,16,1024]{3,2,1,0:T(8,128)(2,1)}, u32[]{:S(2)}, u32[]{:S(2)}) %all-to-all-start) | async-done | bytes 4194336 | tf_op jit(solution)/shard_map/all_to_all | solution.py:101
  184.8 7.9 %fusion.23 = bf16[16,8,16,128]{3,2,1,0:T(8,128)(2,1)S(1)} fusion(bf16[16,8,16,1024]{3,2,1,0:T(8,128)(2,1)} %all-to-all-done, bf16[512,512]{1,0:T(8,128)(2,1)S(1)} %get-tuple-element.8, bf16[512,512]{1,0:T(8,128)(2,1)S(1)} %fusion.64, bf16[512,512]{1,0:T(8,128)(2,1)S(1)} %get-tuple-element.7, bf16[512,64]{1,0:T(8,128)(2,1)S(1)} %bitcast.105, ...), kind=kOutput, calls=%fused_computation.24 | convolution fusion | flops 4843634688 | bytes 6488064 | tf_op jit(solution)/shard_map/smrw,wv->smrv/dot_general | solution.py:105
  192.9 33.7 %all_to_all.10 = bf16[16,8,16,128]{3,1,2,0:T(8,128)(2,1)S(1)} all-to-all(bf16[16,8,16,128]{3,1,2,0:T(8,128)(2,1)S(1)} %copy.57), channel_id=1, replica_groups=mesh['grp'=2,'bits'=16] {'bits'}, dimensions={0} | all-to-all | bytes 1048576 | tf_op jit(solution)/shard_map/all_to_all | solution.py:108
  227.0 0.6 copy.59
  (41 shorter events, 3.6 us)
Async XLA Ops:
  0.0 79.8 %copy-start.1 = (bf16[4,2,32,512]{3,2,1,0:T(8,128)(2,1)S(1)}, bf16[4,2,32,512]{3,2,1,0:T(8,128)(2,1)}, u32[]{:S(2)}) copy-start(bf16[4,2,32,512]{3,2,1,0:T(8,128)(2,1)} %param.9) | copy-start | bytes 786436
  0.0 9.8 %collective-permute-start = (bf16[4,2,32,512]{3,2,1,0:T(8,128)(2,1)}, bf16[4,2,32,512]{3,2,1,0:T(8,128)(2,1)S(1)}, u32[]{:S(2)}, u32[]{:S(2)}) collective-permute-start(bf16[4,2,32,512]{3,2,1,0:T(8,128)(2,1)} %param.9), channel_id=1, source_target_pairs={{0,1},{1,2},{2,3},{3,4},{4,5},{5,6},{6,7},{7,8},{8,9},{9,10},{10,1... | collective-permute-start | bytes 786440 | tf_op jit(solution)/shard_map/ppermute | solution.py:24
  9.8 8.5 %collective-permute-start.1 = (bf16[4,2,32,512]{3,2,1,0:T(8,128)(2,1)S(1)}, bf16[4,2,32,512]{3,2,1,0:T(8,128)(2,1)S(1)}, u32[]{:S(2)}, u32[]{:S(2)}) collective-permute-start(bf16[4,2,32,512]{3,2,1,0:T(8,128)(2,1)S(1)} %collective-permute-done), channel_id=1, source_target_pairs={{0,1},{1,2},{2,3},{3,4},{4,5},{5,6},{6,7},{7,8},{8,9},{9,10},{10,1... | collective-permute-start | bytes 786440 | tf_op jit(solution)/shard_map/ppermute | solution.py:24
  9.8 8.6 %collective-permute-start.8 = (bf16[4,2,32,512]{3,2,1,0:T(8,128)(2,1)}, bf16[4,2,32,512]{3,2,1,0:T(8,128)(2,1)S(1)}, u32[]{:S(2)}, u32[]{:S(2)}) collective-permute-start(bf16[4,2,32,512]{3,2,1,0:T(8,128)(2,1)} %param.9), channel_id=1, source_target_pairs={{1,0},{2,1},{3,2},{4,3},{5,4},{6,5},{7,6},{8,7},{9,8},{10,9},{11,1... | collective-permute-start | bytes 786440 | tf_op jit(solution)/shard_map/ppermute | solution.py:27
  18.3 8.6 %collective-permute-start.2 = (bf16[4,2,32,512]{3,2,1,0:T(8,128)(2,1)S(1)}, bf16[4,2,32,512]{3,2,1,0:T(8,128)(2,1)S(1)}, u32[]{:S(2)}, u32[]{:S(2)}) collective-permute-start(bf16[4,2,32,512]{3,2,1,0:T(8,128)(2,1)S(1)} %collective-permute-done.1), channel_id=1, source_target_pairs={{0,1},{1,2},{2,3},{3,4},{4,5},{5,6},{6,7},{7,8},{8,9},{9,10},{10,1... | collective-permute-start | bytes 786440 | tf_op jit(solution)/shard_map/ppermute | solution.py:24
  18.5 9.2 %collective-permute-start.9 = (bf16[4,2,32,512]{3,2,1,0:T(8,128)(2,1)S(1)}, bf16[4,2,32,512]{3,2,1,0:T(8,128)(2,1)S(1)}, u32[]{:S(2)}, u32[]{:S(2)}) collective-permute-start(bf16[4,2,32,512]{3,2,1,0:T(8,128)(2,1)S(1)} %collective-permute-done.8), channel_id=1, source_target_pairs={{1,0},{2,1},{3,2},{4,3},{5,4},{6,5},{7,6},{8,7},{9,8},{10,9},{11,1... | collective-permute-start | bytes 786440 | tf_op jit(solution)/shard_map/ppermute | solution.py:27
  26.9 8.6 %collective-permute-start.3 = (bf16[4,2,32,512]{3,2,1,0:T(8,128)(2,1)S(1)}, bf16[4,2,32,512]{3,2,1,0:T(8,128)(2,1)S(1)}, u32[]{:S(2)}, u32[]{:S(2)}) collective-permute-start(bf16[4,2,32,512]{3,2,1,0:T(8,128)(2,1)S(1)} %collective-permute-done.2), channel_id=1, source_target_pairs={{0,1},{1,2},{2,3},{3,4},{4,5},{5,6},{6,7},{7,8},{8,9},{9,10},{10,1... | collective-permute-start | bytes 786440 | tf_op jit(solution)/shard_map/ppermute | solution.py:24
  27.7 10.2 %collective-permute-start.10 = (bf16[4,2,32,512]{3,2,1,0:T(8,128)(2,1)S(1)}, bf16[4,2,32,512]{3,2,1,0:T(8,128)(2,1)S(1)}, u32[]{:S(2)}, u32[]{:S(2)}) collective-permute-start(bf16[4,2,32,512]{3,2,1,0:T(8,128)(2,1)S(1)} %collective-permute-done.9), channel_id=1, source_target_pairs={{1,0},{2,1},{3,2},{4,3},{5,4},{6,5},{7,6},{8,7},{9,8},{10,9},{11,1... | collective-permute-start | bytes 786440 | tf_op jit(solution)/shard_map/ppermute | solution.py:27
  35.5 8.6 %collective-permute-start.4 = (bf16[4,2,32,512]{3,2,1,0:T(8,128)(2,1)S(1)}, bf16[4,2,32,512]{3,2,1,0:T(8,128)(2,1)S(1)}, u32[]{:S(2)}, u32[]{:S(2)}) collective-permute-start(bf16[4,2,32,512]{3,2,1,0:T(8,128)(2,1)S(1)} %collective-permute-done.3), channel_id=1, source_target_pairs={{0,1},{1,2},{2,3},{3,4},{4,5},{5,6},{6,7},{7,8},{8,9},{9,10},{10,1... | collective-permute-start | bytes 786440 | tf_op jit(solution)/shard_map/ppermute | solution.py:24
  37.8 8.3 %collective-permute-start.11 = (bf16[4,2,32,512]{3,2,1,0:T(8,128)(2,1)S(1)}, bf16[4,2,32,512]{3,2,1,0:T(8,128)(2,1)S(1)}, u32[]{:S(2)}, u32[]{:S(2)}) collective-permute-start(bf16[4,2,32,512]{3,2,1,0:T(8,128)(2,1)S(1)} %collective-permute-done.10), channel_id=1, source_target_pairs={{1,0},{2,1},{3,2},{4,3},{5,4},{6,5},{7,6},{8,7},{9,8},{10,9},{11,1... | collective-permute-start | bytes 786440 | tf_op jit(solution)/shard_map/ppermute | solution.py:27
  44.1 17.3 %copy-start.2 = (bf16[4,2,32,512]{3,2,1,0:T(8,128)(2,1)}, bf16[4,2,32,512]{3,2,1,0:T(8,128)(2,1)S(1)}, u32[]{:S(2)}) copy-start(bf16[4,2,32,512]{3,2,1,0:T(8,128)(2,1)S(1)} %collective-permute-done.4) | copy-start | bytes 786436
  44.1 8.6 %collective-permute-start.5 = (bf16[4,2,32,512]{3,2,1,0:T(8,128)(2,1)S(1)}, bf16[4,2,32,512]{3,2,1,0:T(8,128)(2,1)S(1)}, u32[]{:S(2)}, u32[]{:S(2)}) collective-permute-start(bf16[4,2,32,512]{3,2,1,0:T(8,128)(2,1)S(1)} %collective-permute-done.4), channel_id=1, source_target_pairs={{0,1},{1,2},{2,3},{3,4},{4,5},{5,6},{6,7},{7,8},{8,9},{9,10},{10,1... | collective-permute-start | bytes 786440 | tf_op jit(solution)/shard_map/ppermute | solution.py:24
  46.2 8.6 %collective-permute-start.12 = (bf16[4,2,32,512]{3,2,1,0:T(8,128)(2,1)S(1)}, bf16[4,2,32,512]{3,2,1,0:T(8,128)(2,1)}, u32[]{:S(2)}, u32[]{:S(2)}) collective-permute-start(bf16[4,2,32,512]{3,2,1,0:T(8,128)(2,1)S(1)} %collective-permute-done.11), channel_id=1, source_target_pairs={{1,0},{2,1},{3,2},{4,3},{5,4},{6,5},{7,6},{8,7},{9,8},{10,9},{11,1... | collective-permute-start | bytes 786440 | tf_op jit(solution)/shard_map/ppermute | solution.py:27
  52.7 8.7 %copy-start.3 = (bf16[4,2,32,512]{3,2,1,0:T(8,128)(2,1)}, bf16[4,2,32,512]{3,2,1,0:T(8,128)(2,1)S(1)}, u32[]{:S(2)}) copy-start(bf16[4,2,32,512]{3,2,1,0:T(8,128)(2,1)S(1)} %collective-permute-done.5) | copy-start | bytes 786436
  52.7 8.7 %collective-permute-start.6 = (bf16[4,2,32,512]{3,2,1,0:T(8,128)(2,1)S(1)}, bf16[4,2,32,512]{3,2,1,0:T(8,128)(2,1)}, u32[]{:S(2)}, u32[]{:S(2)}) collective-permute-start(bf16[4,2,32,512]{3,2,1,0:T(8,128)(2,1)S(1)} %collective-permute-done.5), channel_id=1, source_target_pairs={{0,1},{1,2},{2,3},{3,4},{4,5},{5,6},{6,7},{7,8},{8,9},{9,10},{10,1... | collective-permute-start | bytes 786440 | tf_op jit(solution)/shard_map/ppermute | solution.py:24
  54.8 9.0 %collective-permute-start.13 = (bf16[4,2,32,512]{3,2,1,0:T(8,128)(2,1)}, bf16[4,2,32,512]{3,2,1,0:T(8,128)(2,1)}, u32[]{:S(2)}, u32[]{:S(2)}) collective-permute-start(bf16[4,2,32,512]{3,2,1,0:T(8,128)(2,1)} %collective-permute-done.12), channel_id=1, source_target_pairs={{1,0},{2,1},{3,2},{4,3},{5,4},{6,5},{7,6},{8,7},{9,8},{10,9},{11,1... | collective-permute-start | bytes 786440 | tf_op jit(solution)/shard_map/ppermute | solution.py:27
  61.4 8.8 %collective-permute-start.7 = (bf16[4,2,32,512]{3,2,1,0:T(8,128)(2,1)}, bf16[4,2,32,512]{3,2,1,0:T(8,128)(2,1)}, u32[]{:S(2)}, u32[]{:S(2)}) collective-permute-start(bf16[4,2,32,512]{3,2,1,0:T(8,128)(2,1)} %collective-permute-done.6), channel_id=1, source_target_pairs={{0,1},{1,2},{2,3},{3,4},{4,5},{5,6},{6,7},{7,8},{8,9},{9,10},{10,1... | collective-permute-start | bytes 786440 | tf_op jit(solution)/shard_map/ppermute | solution.py:24
  63.8 23.0 %collective-permute-start.14 = (bf16[4,2,32,512]{3,2,1,0:T(8,128)(2,1)}, bf16[4,2,32,512]{3,2,1,0:T(8,128)(2,1)S(1)}, u32[]{:S(2)}, u32[]{:S(2)}) collective-permute-start(bf16[4,2,32,512]{3,2,1,0:T(8,128)(2,1)} %collective-permute-done.13), channel_id=1, source_target_pairs={{1,0},{2,1},{3,2},{4,3},{5,4},{6,5},{7,6},{8,7},{9,8},{10,9},{11,1... | collective-permute-start | bytes 786440 | tf_op jit(solution)/shard_map/ppermute | solution.py:27
  102.7 4.9 %copy-start.4 = (bf16[2,512,64]{1,2,0:T(8,128)(2,1)S(1)}, bf16[2,512,64]{1,2,0:T(8,128)(2,1)}, u32[]{:S(2)}) copy-start(bf16[2,512,64]{1,2,0:T(8,128)(2,1)} %param.15) | copy-start | bytes 393220
  102.7 5.2 %copy-start = (bf16[1,2,512,512]{3,2,1,0:T(8,128)(2,1)S(1)}, bf16[1,2,512,512]{3,2,1,0:T(8,128)(2,1)}, u32[]{:S(2)}) copy-start(bf16[1,2,512,512]{3,2,1,0:T(8,128)(2,1)} %param.13) | copy-start | bytes 3145732
  102.7 82.1 %all-to-all-start = ((bf16[16,8,16,1024]{3,2,1,0:T(8,128)(2,1)}), bf16[16,8,16,1024]{3,2,1,0:T(8,128)(2,1)}, u32[]{:S(2)}, u32[]{:S(2)}) async-start(bf16[16,8,16,1024]{3,2,1,0:T(8,128)(2,1)} %copy.54), calls=%async_computation | async-start | bytes 8388608 | tf_op jit(solution)/shard_map/all_to_all | solution.py:101
